TPU v7x, 128 devices: a whole 4x4x4 slice. The times are simulated.
128 devices in a mesh: aux: 4 (over y), tile: 32 (over x, z, core).
Axes of the slice: x: 4, y: 4, z: 4, core: 2. Of those that a mesh axis runs over, the one named last changes fastest.
Arguments:
- integrals: bfloat16 [11904, 8, 2944], P(('aux', 'tile')), may hold values from -0.57421875 to 0.57421875
- coefficients: bfloat16 [2944, 2048], replicated, may hold values from -0.109375 to 0.109375
- owned_tiles: int32 [2, 64], replicated, may hold values from 0 to 63, each once within a row
- pair_list: int32 [2, 64, 4], P(None, 'tile'), may hold values from -1 to 63, as said below
- amplitudes: bfloat16 [2, 64, 4, 128, 128], P(None, 'tile'), may hold values from -0.25 to 0.25
Outputs:
- residual: float32 [2, 64, 128, 128], P(None, 'tile')
Inputs may be any that keep to these rules, and one draw needn't show every extreme that they name: `pair_list`: every live entry of slot s is a slot within 2 of s; the live entries of one slot are distinct; -1 marks an entry dropped by screening.
All inputs are finite; a program needn't handle non-finite values.
Results may differ from a plain program's by a relative error of at most 0.00087.
Values may be sent and summed in bfloat16 or wider, within the bound.
A program may use at most 128 MiB of HBM per device.

v0:
```python
import jax
import jax.numpy as jnp
from jax import lax
from jax.sharding import PartitionSpec as P

NB = 2


def per_device(integrals, coefficients, owned_tiles, pair_list, amplitudes):
    tile_count = lax.axis_size("tile")
    q_rows, occ_all, ao_count = integrals.shape
    virt_count = coefficients.shape[1]
    tile_width = amplitudes.shape[-1]
    virt_tiles = virt_count // tile_width
    per_dev = pair_list.shape[1]
    occ_batch = occ_all // NB
    total_slots = owned_tiles.shape[1]
    first_slot = lax.axis_index("tile") * per_dev
    positions = jnp.arange(3 * per_dev, dtype=jnp.int32)
    results = []
    for occ_group in range(NB):
        int_block = integrals[:, occ_group * occ_batch : (occ_group + 1) * occ_batch, :].reshape(
            q_rows * occ_batch, ao_count
        )
        half_done = jnp.dot(int_block, coefficients, preferred_element_type=jnp.float32).astype(
            jnp.bfloat16
        )
        half_done = half_done.reshape(q_rows, occ_batch * virt_tiles, tile_width)
        ordered = jnp.take(half_done, owned_tiles[occ_group], axis=1)
        zero_pad = jnp.zeros((q_rows, per_dev, tile_width), jnp.bfloat16)
        padded = jnp.concatenate([zero_pad, ordered, zero_pad], axis=1)
        below_part = padded[:, :total_slots].reshape(q_rows, tile_count, per_dev, tile_width)
        middle = ordered.reshape(q_rows, tile_count, per_dev, tile_width)
        above_part = padded[:, 2 * per_dev :].reshape(q_rows, tile_count, per_dev, tile_width)
        bundle = jnp.concatenate([below_part, middle, above_part], axis=2)
        arrived = lax.all_to_all(bundle, "tile", split_axis=1, concat_axis=0, tiled=True)
        extended = arrived.reshape(q_rows * tile_count, 3 * per_dev, tile_width)
        mine = extended[:, per_dev : 2 * per_dev]
        listed = pair_list[occ_group]
        ext_place = listed - (first_slot - per_dev)
        selector = (
            (ext_place[:, :, None] == positions[None, None, :]) & (listed[:, :, None] >= 0)
        ).astype(jnp.float32)
        amp_tiles = amplitudes[occ_group]
        cross_ints = jnp.einsum("qja,qeb->jeab", mine, extended, preferred_element_type=jnp.float32)
        partial_value = jnp.einsum(
            "jke,jeab->jkab", selector, cross_ints, precision=lax.Precision.HIGHEST
        )
        summed = lax.psum(partial_value, "aux")
        residue = jnp.einsum(
            "jkab,jkbc->jac", summed, amp_tiles.astype(jnp.float32), precision=lax.Precision.HIGHEST
        )
        results.append(residue)
    return jnp.stack(results)


def solution(mesh):
    in_specs = (
        P(("aux", "tile"), None, None),
        P(),
        P(),
        P(None, "tile", None),
        P(None, "tile", None, None, None),
    )
    out_specs = P(None, "tile", None, None)
    return jax.shard_map(
        per_device, mesh=mesh, in_specs=in_specs, out_specs=out_specs, check_vma=False
    )
```

profile of v0, /device:TPU:96, one launch (start us, length us, event | category | flops | bytes accessed | tf_op | source)
XLA Modules:
  0.0 285.0 jit_solution(10070424365951236372)
XLA Ops:
  6.5 0.8 compare_and_fusion.1
  7.3 6.6 %fusion.28 = (bf16[93,4,2944]{2,1,0:T(4,128)(2,1)}, bf16[93,4,2944]{2,1,0:T(4,128)(2,1)S(1)}) fusion(bf16[93,8,2944]{2,1,0:T(8,128)(2,1)} %param.7), kind=kLoop, calls=%fused_computation.51 | loop fusion | bytes 8761344 | tf_op jit(solution)/shard_map/slice | solution.py:22
  13.9 4.4 %reshape.75 = bf16[372,2944]{1,0:T(8,128)(2,1)} reshape(bf16[93,4,2944]{2,1,0:T(4,128)(2,1)} %get-tuple-element.12) | data formatting | bytes 4380672 | tf_op jit(solution)/shard_map/reshape | solution.py:22
  18.3 11.2 %convolution_convert_fusion.1 = bf16[372,2048]{1,0:T(8,128)(2,1)} fusion(bf16[372,2944]{1,0:T(8,128)(2,1)} %reshape.75, bf16[2944,2048]{1,0:T(8,128)(2,1)} %param.8), kind=kOutput, calls=%fused_computation.9 | convolution fusion | flops 4486569984 | bytes 15772672 | tf_op jit(solution)/shard_map/dot_general | solution.py:25
  29.5 3.7 %reshape.76 = bf16[93,64,128]{2,1,0:T(8,128)(2,1)} reshape(bf16[372,2048]{1,0:T(8,128)(2,1)} %convolution_convert_fusion.1) | data formatting | bytes 3047424 | tf_op jit(solution)/shard_map/reshape | solution.py:28
  33.2 3.6 %copy.14 = bf16[93,64,128]{2,0,1:T(8,128)(2,1)} copy(bf16[93,64,128]{2,1,0:T(8,128)(2,1)} %reshape.76) | data formatting | bytes 3047424 | tf_op jit(solution)/shard_map/reshape | solution.py:28
  36.8 2.6 reshape.81
  39.4 10.0 %convolution_convert_fusion = bf16[372,2048]{1,0:T(8,128)(2,1)S(1)} fusion(bf16[372,2944]{1,0:T(8,128)(2,1)} %reshape.81, bf16[2944,2048]{1,0:T(8,128)(2,1)} %param.8), kind=kOutput, calls=%fused_computation.8 | convolution fusion | flops 4486569984 | bytes 15772672 | tf_op jit(solution)/shard_map/dot_general | solution.py:25
  49.4 1.8 reshape.82
  51.3 0.0 copy-start
  51.3 2.5 copy.18
  53.8 0.0 copy-done
  53.8 1.9 gather_fusion
  55.7 1.9 gather_fusion.1
  57.6 2.2 broadcast_select_fusion
  59.8 0.4 pad_slice_fusion.3
  60.3 2.5 pad_maximum_fusion
  62.7 7.2 %all-to-all-start = ((bf16[93,32,6,128]{3,0,2,1:T(8,128)(2,1)}), bf16[93,32,6,128]{3,0,2,1:T(8,128)(2,1)}, u32[]{:S(2)}, u32[]{:S(2)}) async-start(bf16[93,32,6,128]{3,0,2,1:T(8,128)(2,1)} %pad_maximum_fusion), calls=%async_computation | async-start | bytes 9437184 | tf_op jit(solution)/shard_map/all_to_all | solution.py:36
  69.9 0.4 pad_slice_fusion.1
  70.3 2.4 pad_maximum_fusion.1
  72.8 0.0 copy-start.2
  72.8 54.5 %all-to-all-done = bf16[93,32,6,128]{3,0,2,1:T(8,128)(2,1)} async-done(((bf16[93,32,6,128]{3,0,2,1:T(8,128)(2,1)}), bf16[93,32,6,128]{3,0,2,1:T(8,128)(2,1)}, u32[]{:S(2)}, u32[]{:S(2)}) %all-to-all-start) | async-done | bytes 4571168 | tf_op jit(solution)/shard_map/all_to_all | solution.py:36
  127.3 8.9 %all-to-all-start.1 = ((bf16[93,32,6,128]{3,0,2,1:T(8,128)(2,1)}), bf16[93,32,6,128]{3,0,2,1:T(8,128)(2,1)}, u32[]{:S(2)}, u32[]{:S(2)}) async-start(bf16[93,32,6,128]{3,0,2,1:T(8,128)(2,1)} %pad_maximum_fusion.1), calls=%async_computation.1 | async-start | bytes 9437184 | tf_op jit(solution)/shard_map/all_to_all | solution.py:36
  136.1 0.0 all-reduce.7.cloned.1.call-start
  136.2 0.0 copy-done.2
  136.2 5.5 %copy.15 = bf16[32,93,1,6,128]{4,1,0,3,2:T(8,128)(2,1)} copy(bf16[32,93,1,6,128]{4,1,3,0,2:T(8,128)(2,1)} %bitcast.10) | data formatting | bytes 9142272 | tf_op jit(solution)/shard_map/all_to_all | solution.py:36
  141.7 7.4 %reshape.109 = bf16[2976,6,128,1]{2,0,1,3:T(8,128)(2,1)} reshape(bf16[32,93,1,6,128]{4,1,0,3,2:T(8,128)(2,1)} %copy.15) | data formatting | bytes 9142272 | tf_op jit(solution)/shard_map/reshape | solution.py:37
  149.1 7.3 %reshape.80 = bf16[2976,6,128]{2,0,1:T(8,128)(2,1)} reshape(bf16[32,93,1,6,128]{4,1,0,3,2:T(8,128)(2,1)} %copy.15) | data formatting | bytes 9142272 | tf_op jit(solution)/shard_map/reshape | solution.py:37
  156.5 37.0 %all-to-all-done.1 = bf16[93,32,6,128]{3,0,2,1:T(8,128)(2,1)} async-done(((bf16[93,32,6,128]{3,0,2,1:T(8,128)(2,1)}), bf16[93,32,6,128]{3,0,2,1:T(8,128)(2,1)}, u32[]{:S(2)}, u32[]{:S(2)}) %all-to-all-start.1) | async-done | bytes 4571168 | tf_op jit(solution)/shard_map/all_to_all | solution.py:36
  193.5 5.5 %copy.19 = bf16[32,93,1,6,128]{4,1,0,3,2:T(8,128)(2,1)} copy(bf16[32,93,1,6,128]{4,1,3,0,2:T(8,128)(2,1)} %bitcast.28) | data formatting | bytes 9142272 | tf_op jit(solution)/shard_map/all_to_all | solution.py:36
  199.0 7.4 %reshape.113 = bf16[2976,6,128,1]{2,0,1,3:T(8,128)(2,1)} reshape(bf16[32,93,1,6,128]{4,1,0,3,2:T(8,128)(2,1)} %copy.19) | data formatting | bytes 9142272 | tf_op jit(solution)/shard_map/reshape | solution.py:37
  206.3 7.4 %reshape.86 = bf16[2976,6,128]{2,0,1:T(8,128)(2,1)} reshape(bf16[32,93,1,6,128]{4,1,0,3,2:T(8,128)(2,1)} %copy.19) | data formatting | bytes 9142272 | tf_op jit(solution)/shard_map/reshape | solution.py:37
  213.7 4.2 %fusion.4 = f32[2,6,128,128]{2,3,0,1:T(8,128)S(1)} fusion(bf16[2976,6,128]{2,0,1:T(8,128)(2,1)} %reshape.80, bf16[2976,6,128,1]{2,0,1,3:T(8,128)(2,1)} %reshape.109), kind=kOutput, calls=%fused_computation.18 | convolution fusion | flops 1170210816 | bytes 6881280 | tf_op jit(solution)/shard_map/qja,qeb->jeab/dot_general | solution.py:45
  217.9 0.4 copy.16
  218.3 4.2 %fusion.7 = f32[2,6,128,128]{2,3,0,1:T(8,128)S(1)} fusion(bf16[2976,6,128]{2,0,1:T(8,128)(2,1)} %reshape.86, bf16[2976,6,128,1]{2,0,1,3:T(8,128)(2,1)} %reshape.113), kind=kOutput, calls=%fused_computation.19 | convolution fusion | flops 1170210816 | bytes 6881280 | tf_op jit(solution)/shard_map/qja,qeb->jeab/dot_general | solution.py:45
  222.5 0.4 copy.20
  222.9 0.0 copy-start.1
  222.9 1.5 fusion.18
  224.4 1.5 fusion.22
  225.8 0.0 all-reduce.7.cloned.1.call-update
  225.8 48.7 %all-reduce.7.cloned.1.call-done = (f32[2,4,128,128]{3,1,2,0:T(4,128)}, f32[2,4,128,128]{3,1,2,0:T(4,128)}) async-done(((f32[2,4,128,128]{3,1,2,0:T(4,128)}, f32[2,4,128,128]{3,1,2,0:T(4,128)}), (f32[2,4,128,128]{3,1,2,0:T(4,128)}, f32[2,4,128,128]{3,1,2,0:T(4,128)})) %all-reduce.7.cloned.1.call-update) | async-done | bytes 1048592 | tf_op jit(solution)/shard_map/psum | solution.py:49
  274.5 0.0 copy-done.1
  274.5 1.4 convolution_bitcast_fusion
  276.0 1.4 convolution_bitcast_fusion.1
  277.4 0.7 pad_maximum_fusion.2
  (4 shorter events, 0.0 us)
Async XLA Ops:
  51.3 2.5 copy-start
  62.7 64.5 %all-to-all-start = ((bf16[93,32,6,128]{3,0,2,1:T(8,128)(2,1)}), bf16[93,32,6,128]{3,0,2,1:T(8,128)(2,1)}, u32[]{:S(2)}, u32[]{:S(2)}) async-start(bf16[93,32,6,128]{3,0,2,1:T(8,128)(2,1)} %pad_maximum_fusion), calls=%async_computation | async-start | bytes 9437184 | tf_op jit(solution)/shard_map/all_to_all | solution.py:36
  72.8 63.4 %copy-start.2 = (s32[2,2,4]{2,1,0:T(2,128)S(1)}, s32[2,2,4]{2,1,0:T(2,128)}, u32[]{:S(2)}) copy-start(s32[2,2,4]{2,1,0:T(2,128)} %param.10) | copy-start | bytes 196
  127.3 66.2 %all-to-all-start.1 = ((bf16[93,32,6,128]{3,0,2,1:T(8,128)(2,1)}), bf16[93,32,6,128]{3,0,2,1:T(8,128)(2,1)}, u32[]{:S(2)}, u32[]{:S(2)}) async-start(bf16[93,32,6,128]{3,0,2,1:T(8,128)(2,1)} %pad_maximum_fusion.1), calls=%async_computation.1 | async-start | bytes 9437184 | tf_op jit(solution)/shard_map/all_to_all | solution.py:36
  136.1 138.4 %all-reduce.7.cloned.1.call-start = ((), (), s32[]{:S(2)}) async-start(), calls=%async_computation.2 | async-start | bytes 2097152 | tf_op jit(solution)/shard_map/psum | solution.py:49
  222.9 51.6 %copy-start.1 = (bf16[2,2,4,128,128]{4,3,2,1,0:T(8,128)(2,1)S(1)}, bf16[2,2,4,128,128]{4,3,2,1,0:T(8,128)(2,1)}, u32[]{:S(2)}) copy-start(bf16[2,2,4,128,128]{4,3,2,1,0:T(8,128)(2,1)} %param.11) | copy-start | bytes 1572868
Sparse Core Ops, SparseCore 0:
  226.0 48.5 all-reduce.6
where the time goes:
time: 287 us; the launch traced here: 285 us
  waiting for transfers between devices  140 us (49%)
  local copies, waits for them, and re-layouts  71.2 us (25%)
  matrix products  35.3 us (12%)
  starting transfers between devices  16.1 us (6%)
  between operations  13.5 us (5%)
  other arithmetic  8.62 us (3%)
    all_to_all x2, waiting for transfers between devices, per_device(): lax.all_to_all(bundle, 'tile', split_axis=1, concat_axis=0, tiled=True)  91.5 us
    psum x1, waiting for transfers between devices, per_device(): summed = lax.psum(partial_value, 'aux')  48.7 us
    reshape x4, local copies, waits for them, and re-layouts, per_device(): extended = arrived.reshape(q_rows * tile_count, 3 * per_dev, tile_width)  29.5 us
    dot_general x2, matrix products, per_device(): jnp.dot(int_block, coefficients, preferred_element_type=jnp.float32)  21.2 us
    all_to_all x2, starting transfers between devices, per_device(): lax.all_to_all(bundle, 'tile', split_axis=1, concat_axis=0, tiled=True)  16 us
    reshape x4, local copies, waits for them, and re-layouts, per_device(): half_done = half_done.reshape(q_rows, occ_batch * virt_tiles, tile_width)  11.6 us
    all_to_all x2, local copies, waits for them, and re-layouts, per_device(): lax.all_to_all(bundle, 'tile', split_axis=1, concat_axis=0, tiled=True)  11 us
    dot_general x2, matrix products, per_device(): jnp.einsum('qja,qeb->jeab', mine, extended, preferred_element_type=jnp.fl...  8.4 us
  transfers between devices with their start and end apart: 3, of which 3 were waited for; matrix products, arithmetic and copies ran while one was open for 8% of the time, Pallas kernels for 0%

commit v1 on v0

v1 whole, which is shorter than its diff:
```python
import functools

import jax
import jax.numpy as jnp
from jax import lax
from jax.experimental import pallas as pl
from jax.experimental.pallas import tpu as pltpu
from jax.sharding import PartitionSpec as P

MESH = pl.DeviceIdType.MESH
F32 = jnp.float32
BF16 = jnp.bfloat16

NB = 2
T = 128
NT = 64
NOCC = 8
NOFF = 5
BLK = 16
WIN = BLK + 4
CH = 48
NCH = 2
NSRC = 8
CB = 256


def dev(x, y, z, c):
    return (y, x * 8 + z * 2 + c)


def remote(src, dst, ssem, rsem, where):
    return pltpu.make_async_remote_copy(
        src_ref=src, dst_ref=dst, send_sem=ssem, recv_sem=rsem, device_id=where, device_id_type=MESH
    )


def kernel(
    q_rows,
    owned, plist, integ, coef, amp, out,
    lhs, cbuf, acc, ynat, send, recv, rr, amp5, ampbuf, res, rsrecv, ysend, yrecv, fsend,
    lsem, csem, gsend, grecv, f1send, f1recv, f2send, f2recv, rssend, rsrecv_sem, yssend, ysrecv,
    fssend, fsrecv, locsem,
):
    y = lax.axis_index("aux")
    t = lax.axis_index("tile")
    x = t // 8
    z = (t // 2) % 4
    c = t % 2
    l = x * (1 - c) + z * c
    o = z * (1 - c) + x * c
    nblk = coef.shape[1] // CB
    tail = q_rows - CH

    def lhs_copy(h):
        rows = (CH if h == 0 else tail) * NOCC
        return pltpu.make_async_copy(
            integ.at[pl.ds(h * CH * NOCC, rows)], lhs.at[h, pl.ds(0, rows)], lsem.at[h]
        )

    def coef_copy(n):
        return pltpu.make_async_copy(
            coef.at[:, pl.ds(pl.multiple_of(n * CB, CB), CB)], cbuf.at[n], csem.at[n]
        )

    lhs_copy(0).start()
    for n in range(nblk):
        coef_copy(n).start()
    lhs_copy(1).start()

    bar = pltpu.get_barrier_semaphore()

    def greet(k, carry):
        pl.semaphore_signal(bar, inc=1, device_id=(y, (t + k) % 32), device_id_type=MESH)
        return carry

    lax.fori_loop(1, 32, greet, 0)
    for d in range(1, 4):
        for cc in range(2):
            pl.semaphore_signal(bar, inc=1, device_id=dev(x, (y + d) % 4, z, cc), device_id_type=MESH)
            pl.semaphore_signal(bar, inc=1, device_id=dev(z, (y + d) % 4, x, cc), device_id_type=MESH)

    for b in range(NB):
        for j in range(2):
            slot = 2 * t + j
            for off in range(NOFF):
                total = jnp.zeros((T, T), F32)
                for k in range(4):
                    p = plist[(b * 2 + j) * 4 + k]
                    hit = jnp.logical_and(p >= 0, p - slot + 2 == off).astype(F32)
                    total = total + hit * amp[b, j, k].astype(F32)
                amp5[b, j, off] = total.astype(BF16)

    pl.semaphore_wait(bar, 43)

    quarter = pl.ds(pl.multiple_of(y * 32, 32), 32)
    me8 = z * 2 + c
    f1 = []
    for d in range(4):
        f1.append((0, d, dev(x, y, (z + d) % 4, 0), (c == 0) if d == 0 else None))
        f1.append((1, d, dev((x + d) % 4, y, x, 1), ((c == 1) & (z == x)) if d == 0 else None))

    def f1_copies(i):
        b, d, where, is_self = f1[i]
        src = amp5.at[b, :, :, quarter]
        dst = ampbuf.at[pl.ds(me8 * 2, 2), :, quarter]
        far = remote(src, dst, f1send.at[i], f1recv.at[me8], where)
        near = pltpu.make_async_copy(src, dst, f1recv.at[me8])
        return far, near, is_self

    def start_either(copies):
        far, near, is_self = copies
        if is_self is None:
            far.start()
        else:
            @pl.when(is_self)
            def _():
                near.start()

            @pl.when(jnp.logical_not(is_self))
            def _():
                far.start()

    def finish_send(copies):
        far, near, is_self = copies
        if is_self is None:
            far.wait_send()
        else:
            @pl.when(jnp.logical_not(is_self))
            def _():
                far.wait_send()

    for i in range(8):
        start_either(f1_copies(i))

    here = dev(x, y, z, c)

    def half(h, n):
        whole = jnp.dot(lhs[h], cbuf[n], preferred_element_type=F32)
        for a in range(CB // T):
            acc[a] = whole[:, a * T : (a + 1) * T]
        for i in range(NOCC):
            for a in range(CB // T):
                part = acc[a, pl.ds(i, CH, stride=NOCC), :]
                if h == NCH - 1:
                    rows = lax.broadcasted_iota(jnp.int32, (CH, T), 0)
                    part = jnp.where(rows < tail, part, 0.0)
                ynat[i // 4, (i % 4) * 16 + 2 * n + a] = part.astype(BF16)

    def reorder(h):
        for b in range(NB):
            def one(s, carry):
                send[h, b, s] = ynat[b, owned[b * NT + (s + NT - 2) % NT]]
                return carry

            lax.fori_loop(0, NT + 4, one, 0, unroll=4)

    def place(k):
        return pl.ds(pl.multiple_of(k * CH, CH), CH)

    def gather_copies(h):
        out_copies = []
        for d in range(1, 4):
            xd, zd = (x + d) % 4, (z + d) % 4
            for b, at, k, where in (
                (0, xd, x * 2 + c, dev(xd, y, z, 0)),
                (1, zd, z * 2 + c, dev(x, y, zd, 1)),
            ):
                out_copies.append(
                    remote(
                        send.at[h, b, pl.ds(at * BLK, WIN)],
                        recv.at[h, :, place(k)],
                        gsend.at[h, len(out_copies)],
                        grecv.at[h, k],
                        where,
                    )
                )
        out_copies.append(
            remote(
                send.at[h, 1 - c, pl.ds(o * BLK, WIN)],
                recv.at[h, :, place(o * 2 + c)],
                gsend.at[h, 6],
                grecv.at[h, o * 2 + c],
                dev(x, y, z, 1 - c),
            )
        )
        own = pltpu.make_async_copy(
            send.at[h, c, pl.ds(l * BLK, WIN)], recv.at[h, :, place(l * 2 + c)], locsem.at[h]
        )
        return out_copies, own

    def gather_start(h):
        out_copies, own = gather_copies(h)
        for copy in out_copies:
            copy.start()
        own.start()

    def gather_wait(h):
        out_copies, own = gather_copies(h)
        own.wait()

        def arrived(k):
            remote(
                send.at[h, 0, pl.ds(0, WIN)], recv.at[h, :, place(k)], gsend.at[h, 0], grecv.at[h, k], here
            ).wait_recv()

        arrived(l * 2 + 1 - c)
        for d in range(1, 4):
            for cc in range(2):
                arrived(((l + d) % 4) * 2 + cc)

    def pairs(h):
        def one(j, carry):
            mine = jnp.concatenate([recv[h, 2 * j + 2], recv[h, 2 * j + 3]], axis=1)
            others = jnp.concatenate([recv[h, 2 * j + m] for m in range(6)], axis=1)
            got = lax.dot_general(
                mine, others, (((0,), (0,)), ((), ())), preferred_element_type=F32
            )
            if h == 0:
                rr[j] = got
            else:
                rr[j] = rr[j] + got
            return carry

        lax.fori_loop(0, BLK // 2, one, 0)

    def block0(n, carry):
        coef_copy(n).wait()
        half(0, n)
        return carry

    def block1(n, carry):
        half(1, n)
        return carry

    lhs_copy(0).wait()
    lax.fori_loop(0, nblk // 2, block0, 0)

    f2 = []
    for k in range(NSRC):
        remote(
            amp5.at[0, :, :, quarter], ampbuf.at[pl.ds(2 * k, 2), :, quarter], f1send.at[0], f1recv.at[k], here
        ).wait_recv()
    for d in range(1, 4):
        f2.append(
            remote(
                ampbuf.at[:, :, quarter], ampbuf.at[:, :, quarter], f2send.at[d - 1], f2recv.at[d - 1],
                dev(x, (y + d) % 4, z, c),
            )
        )
        f2[-1].start()

    lax.fori_loop(nblk // 2, nblk, block0, 0)
    reorder(0)
    gather_start(0)
    lhs_copy(1).wait()
    lax.fori_loop(0, nblk, block1, 0)
    reorder(1)
    gather_start(1)
    gather_wait(0)
    pairs(0)
    for d in range(1, 4):
        far_quarter = pl.ds(pl.multiple_of(((y + 4 - d) % 4) * 32, 32), 32)
        remote(
            ampbuf.at[:, :, far_quarter], ampbuf.at[:, :, far_quarter], f2send.at[d - 1], f2recv.at[d - 1], here
        ).wait_recv()
    gather_wait(1)
    pairs(1)

    def contract(op):
        for jj in range(2):
            j = op * 2 + jj
            for e in range(2):
                whole = rr[j, pl.ds(e * T, T), pl.ds(e * T, NOFF * T)]
                high = whole.astype(BF16)
                low = (whole - high.astype(F32)).astype(BF16)
                weights = jnp.concatenate([ampbuf[2 * j + e, m] for m in range(NOFF)], axis=0)
                res[2 * j + e] = jnp.dot(high, weights, preferred_element_type=F32) + jnp.dot(
                    low, weights, preferred_element_type=F32
                )

    rs = []
    for d in range(1, 4):
        op = (o + d) % 4
        contract(op)
        rs.append(
            remote(
                res.at[pl.ds(op * 4, 4)], rsrecv.at[d - 1], rssend.at[d - 1], rsrecv_sem.at[d - 1],
                dev((x + d * c) % 4, y, (z + d * (1 - c)) % 4, c),
            )
        )
        rs[-1].start()
    contract(o)
    for copy in rs:
        copy.wait_recv()

    ys = []
    for d in range(1, 5):
        j = (y + d) % 4
        ysend[d - 1] = (res[o * 4 + j] + rsrecv[0, j]) + (rsrecv[1, j] + rsrecv[2, j])
        if d < 4:
            ys.append(
                remote(
                    ysend.at[d - 1], yrecv.at[d - 1], yssend.at[d - 1], ysrecv.at[d - 1],
                    dev(x, j, z, c),
                )
            )
            ys[-1].start()
    for copy in ys:
        copy.wait_recv()
    fsend[...] = (ysend[3] + yrecv[0]) + (yrecv[1] + yrecv[2])

    def final_copies(d):
        dst = out.at[c, y % 2]
        where = dev(l, (y + d) % 4, o, y // 2)
        far = remote(fsend, dst, fssend.at[d], fsrecv.at[c * 2 + y % 2], where)
        near = pltpu.make_async_copy(fsend, dst, fsrecv.at[c * 2 + y % 2])
        is_self = ((y // 2 == c) & (l == x) & (o == z)) if d == 0 else None
        return far, near, is_self

    for d in range(4):
        start_either(final_copies(d))
    for b in range(NB):
        for j in range(2):
            remote(fsend, out.at[b, j], fssend.at[0], fsrecv.at[b * 2 + j], here).wait_recv()

    for i in range(8):
        finish_send(f1_copies(i))
    for copy in f2 + rs + ys:
        copy.wait_send()
    for h in range(NCH):
        for copy in gather_copies(h)[0]:
            copy.wait_send()
    for d in range(4):
        finish_send(final_copies(d))


def per_device(integrals, coefficients, owned_tiles, pair_list, amplitudes):
    q_rows, occ, ao = integrals.shape
    nv = coefficients.shape[1]
    dma = pltpu.SemaphoreType.DMA
    vmem = pl.BlockSpec(memory_space=pltpu.VMEM)
    smem = pl.BlockSpec(memory_space=pltpu.SMEM)
    hbm = pl.BlockSpec(memory_space=pl.ANY)
    return pl.pallas_call(
        functools.partial(kernel, q_rows),
        out_shape=jax.ShapeDtypeStruct((NB, 2, T, T), F32),
        in_specs=[smem, smem, hbm, hbm, vmem],
        out_specs=vmem,
        scratch_shapes=[
            pltpu.VMEM((NCH, CH * NOCC, ao), BF16),
            pltpu.VMEM((nv // CB, ao, CB), BF16),
            pltpu.VMEM((CB // T, CH * NOCC, T), F32),
            pltpu.VMEM((NB, NT, CH, T), BF16),
            pltpu.VMEM((NCH, NB, NT + 4, CH, T), BF16),
            pltpu.VMEM((NCH, WIN, NSRC * CH, T), BF16),
            pltpu.VMEM((BLK // 2, 2 * T, 6 * T), F32),
            pltpu.VMEM((NB, 2, NOFF, T, T), BF16),
            pltpu.VMEM((BLK, NOFF, T, T), BF16),
            pltpu.VMEM((BLK, T, T), F32),
            pltpu.VMEM((3, 4, T, T), F32),
            pltpu.VMEM((4, T, T), F32),
            pltpu.VMEM((3, T, T), F32),
            pltpu.VMEM((T, T), F32),
            dma((NCH,)),
            dma((nv // CB,)),
            dma((NCH, 7)),
            dma((NCH, NSRC)),
            dma((8,)),
            dma((NSRC,)),
            dma((3,)),
            dma((3,)),
            dma((3,)),
            dma((3,)),
            dma((3,)),
            dma((3,)),
            dma((4,)),
            dma((4,)),
            dma((NCH,)),
        ],
        compiler_params=pltpu.CompilerParams(
            collective_id=0, has_side_effects=True, vmem_limit_bytes=60 * 2**20
        ),
        name="residual_kernel",
    )(
        owned_tiles.reshape(-1),
        pair_list.reshape(-1),
        integrals.reshape(q_rows * occ, ao),
        coefficients,
        amplitudes,
    )


def solution(mesh):
    in_specs = (
        P(("aux", "tile"), None, None),
        P(),
        P(),
        P(None, "tile", None),
        P(None, "tile", None, None, None),
    )
    out_specs = P(None, "tile", None, None)
    return jax.shard_map(
        per_device, mesh=mesh, in_specs=in_specs, out_specs=out_specs, check_vma=False
    )
```

time: 287 us -> 80.6 us (0.28)
  the two profiles are of different devices: /device:TPU:96 before, /device:TPU:1 now
where the time goes in v1:
time: 80.6 us; the launch traced here: 80.4 us
  Pallas kernels  76.1 us (94%)
  local copies, waits for them, and re-layouts  4.27 us (5%)
    pallas_call x1, Pallas kernels, per_device(): pl.pallas_call(functools.partial(kernel, q_rows), out_shape=jax.ShapeDtyp...  76.1 us
    unnamed x1, local copies, waits for them, and re-layouts  1.67 us

profile of v1, /device:TPU:1, one launch (start us, length us, event | category | flops | bytes accessed | tf_op | source)
XLA Modules:
  0.0 80.4 jit_solution(890584463684219318)
XLA Ops:
  0.0 1.3 %reshape.9.owned = s32[128]{0:T(128)} reshape(s32[2,64]{1,0:T(2,128)} %param.7) | data formatting | bytes 1024 | tf_op jit(solution)/shard_map/reshape | solution.py:385
  1.3 1.3 %reshape.10.plist = s32[16]{0:T(128)} reshape(s32[2,2,4]{2,1,0:T(2,128)} %param.8) | data formatting | bytes 128 | tf_op jit(solution)/shard_map/reshape | solution.py:386
  2.6 76.1 %residual_kernel.1 = f32[2,2,128,128]{3,2,1,0:T(8,128)} custom-call(s32[128]{0:T(128)} %reshape.9.owned, s32[16]{0:T(128)} %reshape.10.plist, bf16[744,2944]{1,0:T(8,128)(2,1)} %bitcast.1, bf16[2944,2048]{1,0:T(8,128)(2,1)} %coef.1, bf16[2,2,4,128,128]{4,3,2,1,0:T(8,128)(2,1)} %amp.1), custom_call_target="tpu_custom_call" | custom-call | tf_op jit(solution)/shard_map/residual_kernel/pallas_call | solution.py:344
  78.7 1.7 %copy.7 = f32[2,2,128,128]{3,2,1,0:T(8,128)} copy(f32[2,2,128,128]{3,2,1,0:T(8,128)} %residual_kernel.1) | data formatting | bytes 524288

commit v2 on v1

v2 whole, which is shorter than its diff:
```python
import functools

import jax
import jax.numpy as jnp
from jax import lax
from jax.experimental import pallas as pl
from jax.experimental.pallas import tpu as pltpu
from jax.sharding import PartitionSpec as P

MESH = pl.DeviceIdType.MESH
F32 = jnp.float32
BF16 = jnp.bfloat16

NB = 2
T = 128
NT = 64
NOCC = 8
NOFF = 5
BLK = 16
WIN = BLK + 4
CH = 32
NCH = 3
NSRC = 8
CB = 256
QR = T // 4


def dev(x, y, z, c):
    return (y, x * 8 + z * 2 + c)


def remote(src, dst, ssem, rsem, where):
    return pltpu.make_async_remote_copy(
        src_ref=src, dst_ref=dst, send_sem=ssem, recv_sem=rsem, device_id=where, device_id_type=MESH
    )


def kernel(
    q_rows,
    owned, plist, integ, coef, amp, out,
    lhs, cbuf, acc, ynat, send, recv, rr, amp5, ampbuf, res, rsgot, ysend, ygot, fsend,
    lsem, csem, gsend, grecv, f1send, f1recv, f2send, f2recv, rssend, rsrecv, yssend, ysrecv,
    fssend, fsrecv, locsem,
):
    y = lax.axis_index("aux")
    t = lax.axis_index("tile")
    x = t // 8
    z = (t // 2) % 4
    c = t % 2
    l = x * (1 - c) + z * c
    o = z * (1 - c) + x * c
    here = dev(x, y, z, c)
    nblk = coef.shape[1] // CB
    tail = q_rows - (NCH - 1) * CH

    def lhs_copy(h):
        rows = (CH if h < NCH - 1 else tail) * NOCC
        return pltpu.make_async_copy(
            integ.at[pl.ds(h * CH * NOCC, rows)], lhs.at[h, pl.ds(0, rows)], lsem.at[h]
        )

    def coef_copy(n):
        return pltpu.make_async_copy(
            coef.at[:, pl.ds(pl.multiple_of(n * CB, CB), CB)], cbuf.at[n], csem.at[n]
        )

    lhs_copy(0).start()
    for n in range(nblk):
        coef_copy(n).start()
    for h in range(1, NCH):
        lhs_copy(h).start()

    bar = pltpu.get_barrier_semaphore()

    def greet_plane(k, carry):
        pl.semaphore_signal(bar, inc=1, device_id=(y, (t + k) % 32), device_id_type=MESH)
        return carry

    def greet_others(k, carry):
        yy = (y + 1 + k // 8) % 4
        pl.semaphore_signal(bar, inc=1, device_id=(yy, x * 8 + k % 8), device_id_type=MESH)
        pl.semaphore_signal(
            bar, inc=1, device_id=dev((k // 2) % 4, yy, x, k % 2), device_id_type=MESH
        )
        return carry

    lax.fori_loop(1, 32, greet_plane, 0)
    lax.fori_loop(0, 24, greet_others, 0)

    for b in range(NB):
        for j in range(2):
            slot = 2 * t + j
            for off in range(NOFF):
                total = jnp.zeros((T, T), F32)
                for k in range(4):
                    p = plist[b, j, k]
                    hit = jnp.logical_and(p >= 0, p - slot + 2 == off).astype(F32)
                    total = total + hit * amp[b, j, k].astype(F32)
                amp5[b, j, off] = total.astype(BF16)

    def start_either(copies):
        far, near, is_self = copies
        if is_self is None:
            far.start()
        else:

            @pl.when(is_self)
            def _():
                near.start()

            @pl.when(jnp.logical_not(is_self))
            def _():
                far.start()

    def finish_send(copies):
        far, near, is_self = copies
        if is_self is None:
            far.wait_send()
        else:

            @pl.when(jnp.logical_not(is_self))
            def _():
                far.wait_send()

    def quarter_of(yy):
        return pl.ds(pl.multiple_of(yy * QR, QR), QR)

    quarter = quarter_of(y)
    me8 = z * 2 + c

    def f1_copies(b, d):
        src = amp5.at[b, :, :, quarter]
        dst = ampbuf.at[pl.ds(me8 * 2, 2), :, quarter]
        if b == 0:
            where, is_self = dev(x, y, (z + d) % 4, 0), c == 0
        else:
            where, is_self = dev((x + d) % 4, y, x, 1), (c == 1) & (z == x)
        far = remote(src, dst, f1send.at[b, d], f1recv.at[me8], where)
        near = pltpu.make_async_copy(src, dst, f1recv.at[me8])
        return far, near, is_self if d == 0 else None

    def f2_copy(g, d, yy, where):
        part = ampbuf.at[pl.ds(4 * g, 4), :, quarter_of(yy)]
        return remote(part, part, f2send.at[g, d - 1], f2recv.at[g, d - 1], where)

    def f2_start(g):
        for k in (2 * g, 2 * g + 1):
            remote(
                amp5.at[0, :, :, quarter], ampbuf.at[pl.ds(2 * k, 2), :, quarter],
                f1send.at[0, 0], f1recv.at[k], here,
            ).wait_recv()
        for d in range(1, 4):
            f2_copy(g, d, y, dev(x, (y + d) % 4, z, c)).start()

    def half(h, n):
        whole = jnp.dot(lhs[h], cbuf[n], preferred_element_type=F32)
        for a in range(CB // T):
            acc[a] = whole[:, a * T : (a + 1) * T]
        for i in range(NOCC):
            for a in range(CB // T):
                part = acc[a, pl.ds(i, CH, stride=NOCC), :]
                if h == NCH - 1:
                    rows = lax.broadcasted_iota(jnp.int32, (CH, T), 0)
                    part = jnp.where(rows < tail, part, 0.0)
                ynat[i // 4, (i % 4) * 16 + 2 * n + a] = part.astype(BF16)

    def reorder(h):
        for b in range(NB):

            def one(s, carry):
                send[h, b, s] = ynat[b, owned[b, (s + NT - 2) % NT]]
                return carry

            lax.fori_loop(0, NT + 4, one, 0, unroll=4)

    def place(k):
        return pl.ds(pl.multiple_of(k * CH, CH), CH)

    def groups(h):
        return ((0, 8), (8, 4), (12, 4), (16, 4)) if h == NCH - 1 else ((0, WIN),)

    def gather_copies(h, g):
        low, count = groups(h)[g]
        q = h + g
        copies = []
        for d in range(1, 4):
            xd, zd = (x + d) % 4, (z + d) % 4
            for b, at, k, where in (
                (0, xd, x * 2 + c, dev(xd, y, z, 0)),
                (1, zd, z * 2 + c, dev(x, y, zd, 1)),
            ):
                copies.append(
                    remote(
                        send.at[h, b, pl.ds(at * BLK + low, count)],
                        recv.at[h, pl.ds(low, count), place(k)],
                        gsend.at[q, len(copies)],
                        grecv.at[q, k],
                        where,
                    )
                )
        copies.append(
            remote(
                send.at[h, 1 - c, pl.ds(o * BLK + low, count)],
                recv.at[h, pl.ds(low, count), place(o * 2 + c)],
                gsend.at[q, 6],
                grecv.at[q, o * 2 + c],
                dev(x, y, z, 1 - c),
            )
        )
        own = pltpu.make_async_copy(
            send.at[h, c, pl.ds(l * BLK + low, count)],
            recv.at[h, pl.ds(low, count), place(l * 2 + c)],
            locsem.at[q],
        )
        return copies, own

    def gather_start(h):
        for g in range(len(groups(h))):
            copies, own = gather_copies(h, g)
            for copy in copies:
                copy.start()
            own.start()

    def gather_wait(h, g):
        low, count = groups(h)[g]
        q = h + g
        gather_copies(h, g)[1].wait()

        def arrived(k):
            remote(
                send.at[h, 0, pl.ds(low, count)], recv.at[h, pl.ds(low, count), place(k)],
                gsend.at[q, 0], grecv.at[q, k], here,
            ).wait_recv()

        arrived(l * 2 + 1 - c)
        for d in range(1, 4):
            for cc in range(2):
                arrived(((l + d) % 4) * 2 + cc)

    def pairs(h, first, last):
        def one(j, carry):
            mine = jnp.concatenate([recv[h, 2 * j + 2], recv[h, 2 * j + 3]], axis=1)
            others = jnp.concatenate([recv[h, 2 * j + m] for m in range(6)], axis=1)
            got = lax.dot_general(
                mine, others, (((0,), (0,)), ((), ())), preferred_element_type=F32
            )
            if h == 0:
                rr[j] = got
            else:
                rr[j] = rr[j] + got
            return carry

        lax.fori_loop(first, last, one, 0)

    def contract(g):
        for e in range(4):
            j, u = 2 * g + e // 2, e % 2
            whole = rr[j, pl.ds(u * T, T), pl.ds(u * T, NOFF * T)]
            high = whole.astype(BF16)
            low = (whole - high.astype(F32)).astype(BF16)
            weights = jnp.concatenate([ampbuf[4 * g + e, m] for m in range(NOFF)], axis=0)
            res[4 * g + e] = jnp.dot(high, weights, preferred_element_type=F32) + jnp.dot(
                low, weights, preferred_element_type=F32
            )

    def rs_copy(g, d):
        return remote(
            res.at[4 * g + (o + d) % 4], rsgot.at[g, d - 1], rssend.at[g, d - 1], rsrecv.at[g, d - 1],
            dev((x + d * c) % 4, y, (z + d * (1 - c)) % 4, c),
        )

    def y_copy(g, d):
        return remote(
            ysend.at[g, quarter_of((y + d) % 4)], ygot.at[g, d - 1], yssend.at[g, d - 1],
            ysrecv.at[g, d - 1], dev(x, (y + d) % 4, z, c),
        )

    def y_start(g):
        for d in range(1, 4):
            rs_copy(g, d).wait_recv()
        ysend[g] = (res[4 * g + o] + rsgot[g, 0]) + (rsgot[g, 1] + rsgot[g, 2])
        for d in range(1, 4):
            y_copy(g, d).start()

    def final_copies(g, d):
        dst = out.at[c, o % 2, quarter]
        sem = fsrecv.at[c * 8 + (o % 2) * 4 + y]
        far = remote(fsend.at[g], dst, fssend.at[g, d], sem, dev(l, (y + d) % 4, g, o // 2))
        near = pltpu.make_async_copy(fsend.at[g], dst, sem)
        is_self = ((o // 2 == c) & (l == x) & (z == g)) if d == 0 else None
        return far, near, is_self

    def final_start(g):
        for d in range(1, 4):
            y_copy(g, d).wait_recv()
        fsend[g] = (ysend[g, quarter] + ygot[g, 0]) + (ygot[g, 1] + ygot[g, 2])
        for d in range(4):
            start_either(final_copies(g, d))

    def block(h):
        def one(n, carry):
            if h == 0:
                coef_copy(n).wait()
            half(h, n)
            return carry

        return one

    lhs_copy(0).wait()
    lax.fori_loop(0, nblk // 2, block(0), 0)
    pl.semaphore_wait(bar, 31 + 48)
    for d in range(4):
        for b in range(NB):
            start_either(f1_copies(b, d))
    lax.fori_loop(nblk // 2, nblk, block(0), 0)
    reorder(0)
    gather_start(0)
    lhs_copy(1).wait()
    lax.fori_loop(0, nblk, block(1), 0)
    reorder(1)
    gather_start(1)
    for g in range(4):
        f2_start(g)
    lhs_copy(2).wait()
    lax.fori_loop(0, nblk, block(2), 0)
    reorder(2)
    gather_start(2)
    for h in range(NCH - 1):
        gather_wait(h, 0)
        pairs(h, 0, BLK // 2)
    for g in range(6):
        if g < 4:
            gather_wait(NCH - 1, g)
            pairs(NCH - 1, 2 * g, 2 * g + 2)
            for d in range(1, 4):
                f2_copy(g, d, (y + 4 - d) % 4, here).wait_recv()
            contract(g)
            for d in range(1, 4):
                rs_copy(g, d).start()
        if 1 <= g <= 4:
            y_start(g - 1)
        if 2 <= g:
            final_start(g - 2)

    for b in range(NB):
        for j in range(2):
            for yy in range(4):
                remote(
                    fsend.at[0], out.at[b, j, pl.ds(yy * QR, QR)], fssend.at[0, 0],
                    fsrecv.at[b * 8 + j * 4 + yy], here,
                ).wait_recv()

    for d in range(4):
        for b in range(NB):
            finish_send(f1_copies(b, d))
    for h in range(NCH):
        for g in range(len(groups(h))):
            for copy in gather_copies(h, g)[0]:
                copy.wait_send()
    for g in range(4):
        for d in range(1, 4):
            f2_copy(g, d, y, here).wait_send()
            rs_copy(g, d).wait_send()
            y_copy(g, d).wait_send()
        for d in range(4):
            finish_send(final_copies(g, d))


def per_device(integrals, coefficients, owned_tiles, pair_list, amplitudes):
    q_rows, occ, ao = integrals.shape
    nv = coefficients.shape[1]
    dma = pltpu.SemaphoreType.DMA
    vmem = pl.BlockSpec(memory_space=pltpu.VMEM)
    smem = pl.BlockSpec(memory_space=pltpu.SMEM)
    hbm = pl.BlockSpec(memory_space=pl.ANY)
    return pl.pallas_call(
        functools.partial(kernel, q_rows),
        out_shape=jax.ShapeDtypeStruct((NB, 2, T, T), F32),
        in_specs=[smem, smem, hbm, hbm, vmem],
        out_specs=vmem,
        scratch_shapes=[
            pltpu.VMEM((NCH, CH * NOCC, ao), BF16),
            pltpu.VMEM((nv // CB, ao, CB), BF16),
            pltpu.VMEM((CB // T, CH * NOCC, T), F32),
            pltpu.VMEM((NB, NT, CH, T), BF16),
            pltpu.VMEM((NCH, NB, NT + 4, CH, T), BF16),
            pltpu.VMEM((NCH, WIN, NSRC * CH, T), BF16),
            pltpu.VMEM((BLK // 2, 2 * T, 6 * T), F32),
            pltpu.VMEM((NB, 2, NOFF, T, T), BF16),
            pltpu.VMEM((BLK, NOFF, T, T), BF16),
            pltpu.VMEM((BLK, T, T), F32),
            pltpu.VMEM((4, 3, T, T), F32),
            pltpu.VMEM((4, T, T), F32),
            pltpu.VMEM((4, 3, QR, T), F32),
            pltpu.VMEM((4, QR, T), F32),
            dma((NCH,)),
            dma((nv // CB,)),
            dma((NCH + 3, 7)),
            dma((NCH + 3, NSRC)),
            dma((NB, 4)),
            dma((NSRC,)),
            dma((4, 3)),
            dma((4, 3)),
            dma((4, 3)),
            dma((4, 3)),
            dma((4, 3)),
            dma((4, 3)),
            dma((4, 4)),
            dma((16,)),
            dma((NCH + 3,)),
        ],
        compiler_params=pltpu.CompilerParams(
            collective_id=0, has_side_effects=True, vmem_limit_bytes=60 * 2**20
        ),
        name="residual_kernel",
    )(
        owned_tiles,
        pair_list,
        integrals.reshape(q_rows * occ, ao),
        coefficients,
        amplitudes,
    )


def solution(mesh):
    in_specs = (
        P(("aux", "tile"), None, None),
        P(),
        P(),
        P(None, "tile", None),
        P(None, "tile", None, None, None),
    )
    out_specs = P(None, "tile", None, None)
    return jax.shard_map(
        per_device, mesh=mesh, in_specs=in_specs, out_specs=out_specs, check_vma=False
    )
```

time: 80.6 us -> 73.7 us (0.914)
  the two profiles are of different devices: /device:TPU:1 before, /device:TPU:102 now
where the time goes in v2:
time: 73.7 us; the launch traced here: 73.5 us
  Pallas kernels  71.8 us (97%)
  local copies, waits for them, and re-layouts  1.67 us (2%)
    pallas_call x1, Pallas kernels, per_device(): pl.pallas_call(functools.partial(kernel, q_rows), out_shape=jax.ShapeDtyp...  71.8 us
    unnamed x1, local copies, waits for them, and re-layouts  1.67 us

profile of v2, /device:TPU:102, one launch (start us, length us, event | category | flops | bytes accessed | tf_op | source)
XLA Modules:
  0.0 73.5 jit_solution(6124907799056283470)
XLA Ops:
  0.0 71.8 %residual_kernel.1 = f32[2,2,128,128]{3,2,1,0:T(8,128)} custom-call(s32[2,64]{1,0:T(2,128)} %owned.1, s32[2,2,4]{2,1,0:T(2,128)} %plist.1, bf16[744,2944]{1,0:T(8,128)(2,1)} %bitcast.1, bf16[2944,2048]{1,0:T(8,128)(2,1)} %coef.1, bf16[2,2,4,128,128]{4,3,2,1,0:T(8,128)(2,1)} %amp.1), custom_call_target="tpu_custom_call" | custom-call | tf_op jit(solution)/shard_map/residual_kernel/pallas_call | solution.py:376
  71.8 1.7 %copy.7 = f32[2,2,128,128]{3,2,1,0:T(8,128)} copy(f32[2,2,128,128]{3,2,1,0:T(8,128)} %residual_kernel.1) | data formatting | bytes 524288

commit v3 on v2

--- a/solution.py
+++ b/solution.py
@@ -18,8 +18,10 @@
 NOFF = 5
 BLK = 16
 WIN = BLK + 4
-CH = 32
-NCH = 3
+CHUNKS = (32, 32, 32)
+START = (0, 32, 64)
+NCH = len(CHUNKS)
+ROWS = sum(CHUNKS)
 NSRC = 8
 CB = 256
 QR = T // 4
@@ -38,7 +40,7 @@
 def kernel(
     q_rows,
     owned, plist, integ, coef, amp, out,
-    lhs, cbuf, acc, ynat, send, recv, rr, amp5, ampbuf, res, rsgot, ysend, ygot, fsend,
+    lhs, cbuf, acc, ynat, send, recv, rr, offs, offbuf, amp5, ampbuf, res, rsgot, ysend, ygot, fsend,
     lsem, csem, gsend, grecv, f1send, f1recv, f2send, f2recv, rssend, rsrecv, yssend, ysrecv,
     fssend, fsrecv, locsem,
 ):
@@ -51,13 +53,11 @@
     o = z * (1 - c) + x * c
     here = dev(x, y, z, c)
     nblk = coef.shape[1] // CB
-    tail = q_rows - (NCH - 1) * CH
+    tail = q_rows - START[-1]
 
     def lhs_copy(h):
-        rows = (CH if h < NCH - 1 else tail) * NOCC
-        return pltpu.make_async_copy(
-            integ.at[pl.ds(h * CH * NOCC, rows)], lhs.at[h, pl.ds(0, rows)], lsem.at[h]
-        )
+        part = pl.ds(START[h] * NOCC, (CHUNKS[h] if h < NCH - 1 else tail) * NOCC)
+        return pltpu.make_async_copy(integ.at[part], lhs.at[part], lsem.at[h])
 
     def coef_copy(n):
         return pltpu.make_async_copy(
@@ -72,31 +72,26 @@
 
     bar = pltpu.get_barrier_semaphore()
 
-    def greet_plane(k, carry):
-        pl.semaphore_signal(bar, inc=1, device_id=(y, (t + k) % 32), device_id_type=MESH)
+    def greet(where):
+        pl.semaphore_signal(bar, inc=1, device_id=where, device_id_type=MESH)
+
+    def greet_sources(k, carry):
+        p, cc = k // 2, k % 2
+        greet(dev(x * c + p * (1 - c), y, z * (1 - c) + p * c, cc))
+        greet(dev(l, y, p, cc))
         return carry
 
-    def greet_others(k, carry):
-        yy = (y + 1 + k // 8) % 4
-        pl.semaphore_signal(bar, inc=1, device_id=(yy, x * 8 + k % 8), device_id_type=MESH)
-        pl.semaphore_signal(
-            bar, inc=1, device_id=dev((k // 2) % 4, yy, x, k % 2), device_id_type=MESH
-        )
-        return carry
-
-    lax.fori_loop(1, 32, greet_plane, 0)
-    lax.fori_loop(0, 24, greet_others, 0)
+    lax.fori_loop(0, 8, greet_sources, 0)
+    for d in range(1, 4):
+        greet(dev((x + d * c) % 4, y, (z + d * (1 - c)) % 4, c))
+        greet(dev(x, (y + d) % 4, z, c))
 
     for b in range(NB):
         for j in range(2):
-            slot = 2 * t + j
-            for off in range(NOFF):
-                total = jnp.zeros((T, T), F32)
-                for k in range(4):
-                    p = plist[b, j, k]
-                    hit = jnp.logical_and(p >= 0, p - slot + 2 == off).astype(F32)
-                    total = total + hit * amp[b, j, k].astype(F32)
-                amp5[b, j, off] = total.astype(BF16)
+            for k in range(4):
+                p = plist[b, j, k]
+                off = jnp.where(p >= 0, p - (2 * t + j) + 2, -1).astype(F32)
+                offs[b, pl.ds(4 * j + k, 1)] = jnp.full((1, T), off, F32)
 
     def start_either(copies):
         far, near, is_self = copies
@@ -129,15 +124,20 @@
     me8 = z * 2 + c
 
     def f1_copies(b, d):
-        src = amp5.at[b, :, :, quarter]
+        src = amp.at[b, :, :, quarter]
         dst = ampbuf.at[pl.ds(me8 * 2, 2), :, quarter]
         if b == 0:
             where, is_self = dev(x, y, (z + d) % 4, 0), c == 0
         else:
             where, is_self = dev((x + d) % 4, y, x, 1), (c == 1) & (z == x)
-        far = remote(src, dst, f1send.at[b, d], f1recv.at[me8], where)
-        near = pltpu.make_async_copy(src, dst, f1recv.at[me8])
-        return far, near, is_self if d == 0 else None
+        is_self = is_self if d == 0 else None
+        far = remote(src, dst, f1send.at[0, b, d], f1recv.at[0, me8], where)
+        near = pltpu.make_async_copy(src, dst, f1recv.at[0, me8])
+        far_offs = remote(
+            offs.at[b], offbuf.at[me8], f1send.at[1, b, d], f1recv.at[1, me8], where
+        )
+        near_offs = pltpu.make_async_copy(offs.at[b], offbuf.at[me8], f1recv.at[1, me8])
+        return (far_offs, near_offs, is_self), (far, near, is_self)
 
     def f2_copy(g, d, yy, where):
         part = ampbuf.at[pl.ds(4 * g, 4), :, quarter_of(yy)]
@@ -146,35 +146,62 @@
     def f2_start(g):
         for k in (2 * g, 2 * g + 1):
             remote(
-                amp5.at[0, :, :, quarter], ampbuf.at[pl.ds(2 * k, 2), :, quarter],
-                f1send.at[0, 0], f1recv.at[k], here,
+                offs.at[0], offbuf.at[k], f1send.at[1, 0, 0], f1recv.at[1, k], here
             ).wait_recv()
+            remote(
+                amp.at[0, :, :, quarter], ampbuf.at[pl.ds(2 * k, 2), :, quarter],
+                f1send.at[0, 0, 0], f1recv.at[0, k], here,
+            ).wait_recv()
         for d in range(1, 4):
             f2_copy(g, d, y, dev(x, (y + d) % 4, z, c)).start()
 
+    def f2_wait(g):
+        for d in range(1, 4):
+            f2_copy(g, d, (y + 4 - d) % 4, here).wait_recv()
+
+    def by_offset(g):
+        for e in range(4):
+            k8, r = 2 * g + e // 2, 4 * (e % 2)
+            for m in range(NOFF):
+                total = None
+                for k in range(4):
+                    row = offbuf[k8, pl.ds(r + k, 1)]
+                    hit = jnp.where(row == float(m), 1.0, 0.0).astype(BF16)
+                    term = jnp.broadcast_to(hit, (T, T)) * ampbuf[4 * g + e, k]
+                    total = term if total is None else total + term
+                amp5[4 * g + e, pl.ds(m * T, T)] = total
+
     def half(h, n):
-        whole = jnp.dot(lhs[h], cbuf[n], preferred_element_type=F32)
+        rows_h = CHUNKS[h]
+        mine = lhs[pl.ds(START[h] * NOCC, rows_h * NOCC)]
+        whole = jnp.dot(mine, cbuf[n], preferred_element_type=F32)
         for a in range(CB // T):
-            acc[a] = whole[:, a * T : (a + 1) * T]
+            acc[a, pl.ds(0, rows_h * NOCC)] = whole[:, a * T : (a + 1) * T]
         for i in range(NOCC):
             for a in range(CB // T):
-                part = acc[a, pl.ds(i, CH, stride=NOCC), :]
+                part = acc[a, pl.ds(i, rows_h, stride=NOCC), :]
                 if h == NCH - 1:
-                    rows = lax.broadcasted_iota(jnp.int32, (CH, T), 0)
+                    rows = lax.broadcasted_iota(jnp.int32, (rows_h, T), 0)
                     part = jnp.where(rows < tail, part, 0.0)
-                ynat[i // 4, (i % 4) * 16 + 2 * n + a] = part.astype(BF16)
+                ynat[i // 4, (i % 4) * 16 + 2 * n + a, pl.ds(0, rows_h)] = part.astype(BF16)
 
     def reorder(h):
         for b in range(NB):
 
             def one(s, carry):
-                send[h, b, s] = ynat[b, owned[b, (s + NT - 2) % NT]]
+                send[b, s, pl.ds(START[h], CHUNKS[h])] = ynat[
+                    b, owned[b, (s + NT - 2) % NT], pl.ds(0, CHUNKS[h])
+                ]
                 return carry
 
             lax.fori_loop(0, NT + 4, one, 0, unroll=4)
 
-    def place(k):
-        return pl.ds(pl.multiple_of(k * CH, CH), CH)
+    def place(h, k):
+        rows_h = CHUNKS[h]
+        return pl.ds(pl.multiple_of(START[h] * NSRC + k * rows_h, 16), rows_h)
+
+    def part(h):
+        return pl.ds(START[h], CHUNKS[h])
 
     def groups(h):
         return ((0, 8), (8, 4), (12, 4), (16, 4)) if h == NCH - 1 else ((0, WIN),)
@@ -191,8 +218,8 @@
             ):
                 copies.append(
                     remote(
-                        send.at[h, b, pl.ds(at * BLK + low, count)],
-                        recv.at[h, pl.ds(low, count), place(k)],
+                        send.at[b, pl.ds(at * BLK + low, count), part(h)],
+                        recv.at[pl.ds(low, count), place(h, k)],
                         gsend.at[q, len(copies)],
                         grecv.at[q, k],
                         where,
@@ -200,16 +227,16 @@
                 )
         copies.append(
             remote(
-                send.at[h, 1 - c, pl.ds(o * BLK + low, count)],
-                recv.at[h, pl.ds(low, count), place(o * 2 + c)],
+                send.at[1 - c, pl.ds(o * BLK + low, count), part(h)],
+                recv.at[pl.ds(low, count), place(h, o * 2 + c)],
                 gsend.at[q, 6],
                 grecv.at[q, o * 2 + c],
                 dev(x, y, z, 1 - c),
             )
         )
         own = pltpu.make_async_copy(
-            send.at[h, c, pl.ds(l * BLK + low, count)],
-            recv.at[h, pl.ds(low, count), place(l * 2 + c)],
+            send.at[c, pl.ds(l * BLK + low, count), part(h)],
+            recv.at[pl.ds(low, count), place(h, l * 2 + c)],
             locsem.at[q],
         )
         return copies, own
@@ -228,7 +255,7 @@
 
         def arrived(k):
             remote(
-                send.at[h, 0, pl.ds(low, count)], recv.at[h, pl.ds(low, count), place(k)],
+                send.at[0, pl.ds(low, count), part(h)], recv.at[pl.ds(low, count), place(h, k)],
                 gsend.at[q, 0], grecv.at[q, k], here,
             ).wait_recv()
 
@@ -237,14 +264,16 @@
             for cc in range(2):
                 arrived(((l + d) % 4) * 2 + cc)
 
-    def pairs(h, first, last):
+    def pairs(low, high, first, last):
+        rows = pl.ds(low * NSRC, (high - low) * NSRC)
+
         def one(j, carry):
-            mine = jnp.concatenate([recv[h, 2 * j + 2], recv[h, 2 * j + 3]], axis=1)
-            others = jnp.concatenate([recv[h, 2 * j + m] for m in range(6)], axis=1)
+            mine = jnp.concatenate([recv[2 * j + 2, rows], recv[2 * j + 3, rows]], axis=1)
+            others = jnp.concatenate([recv[2 * j + m, rows] for m in range(6)], axis=1)
             got = lax.dot_general(
                 mine, others, (((0,), (0,)), ((), ())), preferred_element_type=F32
             )
-            if h == 0:
+            if low == 0:
                 rr[j] = got
             else:
                 rr[j] = rr[j] + got
@@ -258,7 +287,7 @@
             whole = rr[j, pl.ds(u * T, T), pl.ds(u * T, NOFF * T)]
             high = whole.astype(BF16)
             low = (whole - high.astype(F32)).astype(BF16)
-            weights = jnp.concatenate([ampbuf[4 * g + e, m] for m in range(NOFF)], axis=0)
+            weights = amp5[4 * g + e]
             res[4 * g + e] = jnp.dot(high, weights, preferred_element_type=F32) + jnp.dot(
                 low, weights, preferred_element_type=F32
             )
@@ -307,40 +336,41 @@
         return one
 
     lhs_copy(0).wait()
-    lax.fori_loop(0, nblk // 2, block(0), 0)
-    pl.semaphore_wait(bar, 31 + 48)
+    lax.fori_loop(0, 1, block(0), 0)
+    pl.semaphore_wait(bar, 22)
     for d in range(4):
         for b in range(NB):
-            start_either(f1_copies(b, d))
-    lax.fori_loop(nblk // 2, nblk, block(0), 0)
+            for one in f1_copies(b, d):
+                start_either(one)
+    lax.fori_loop(1, nblk, block(0), 0)
     reorder(0)
     gather_start(0)
     lhs_copy(1).wait()
-    lax.fori_loop(0, nblk, block(1), 0)
+    lax.fori_loop(0, nblk // 2, block(1), 0)
+    for g in range(4):
+        f2_start(g)
+    lax.fori_loop(nblk // 2, nblk, block(1), 0)
     reorder(1)
     gather_start(1)
-    for g in range(4):
-        f2_start(g)
     lhs_copy(2).wait()
     lax.fori_loop(0, nblk, block(2), 0)
     reorder(2)
     gather_start(2)
     for h in range(NCH - 1):
         gather_wait(h, 0)
-        pairs(h, 0, BLK // 2)
-    for g in range(6):
-        if g < 4:
-            gather_wait(NCH - 1, g)
-            pairs(NCH - 1, 2 * g, 2 * g + 2)
-            for d in range(1, 4):
-                f2_copy(g, d, (y + 4 - d) % 4, here).wait_recv()
-            contract(g)
-            for d in range(1, 4):
-                rs_copy(g, d).start()
-        if 1 <= g <= 4:
-            y_start(g - 1)
-        if 2 <= g:
-            final_start(g - 2)
+    pairs(0, START[-1], 0, BLK // 2)
+    for g in range(4):
+        f2_wait(g)
+        by_offset(g)
+        gather_wait(NCH - 1, g)
+        pairs(START[-1], ROWS, 2 * g, 2 * g + 2)
+        contract(g)
+        for d in range(1, 4):
+            rs_copy(g, d).start()
+    for g in range(4):
+        y_start(g)
+    for g in range(4):
+        final_start(g)
 
     for b in range(NB):
         for j in range(2):
@@ -352,7 +382,8 @@
 
     for d in range(4):
         for b in range(NB):
-            finish_send(f1_copies(b, d))
+            for one in f1_copies(b, d):
+                finish_send(one)
     for h in range(NCH):
         for g in range(len(groups(h))):
             for copy in gather_copies(h, g)[0]:
@@ -379,15 +410,17 @@
         in_specs=[smem, smem, hbm, hbm, vmem],
         out_specs=vmem,
         scratch_shapes=[
-            pltpu.VMEM((NCH, CH * NOCC, ao), BF16),
+            pltpu.VMEM((ROWS * NOCC, ao), BF16),
             pltpu.VMEM((nv // CB, ao, CB), BF16),
-            pltpu.VMEM((CB // T, CH * NOCC, T), F32),
-            pltpu.VMEM((NB, NT, CH, T), BF16),
-            pltpu.VMEM((NCH, NB, NT + 4, CH, T), BF16),
-            pltpu.VMEM((NCH, WIN, NSRC * CH, T), BF16),
+            pltpu.VMEM((CB // T, max(CHUNKS) * NOCC, T), F32),
+            pltpu.VMEM((NB, NT, max(CHUNKS), T), BF16),
+            pltpu.VMEM((NB, NT + 4, ROWS, T), BF16),
+            pltpu.VMEM((WIN, NSRC * ROWS, T), BF16),
             pltpu.VMEM((BLK // 2, 2 * T, 6 * T), F32),
-            pltpu.VMEM((NB, 2, NOFF, T, T), BF16),
-            pltpu.VMEM((BLK, NOFF, T, T), BF16),
+            pltpu.VMEM((NB, 8, T), F32),
+            pltpu.VMEM((NSRC, 8, T), F32),
+            pltpu.VMEM((BLK, NOFF * T, T), BF16),
+            pltpu.VMEM((BLK, 4, T, T), BF16),
             pltpu.VMEM((BLK, T, T), F32),
             pltpu.VMEM((4, 3, T, T), F32),
             pltpu.VMEM((4, T, T), F32),
@@ -397,8 +430,8 @@
             dma((nv // CB,)),
             dma((NCH + 3, 7)),
             dma((NCH + 3, NSRC)),
-            dma((NB, 4)),
-            dma((NSRC,)),
+            dma((2, NB, 4)),
+            dma((2, NSRC)),
             dma((4, 3)),
             dma((4, 3)),
             dma((4, 3)),

time: 73.7 us -> 61.1 us (0.83)
  the two profiles are of different devices: /device:TPU:102 before, /device:TPU:96 now
where the time goes in v3:
time: 61.1 us; the launch traced here: 60.8 us
  Pallas kernels  59.1 us (97%)
  local copies, waits for them, and re-layouts  1.67 us (3%)
    pallas_call x1, Pallas kernels, per_device(): pl.pallas_call(functools.partial(kernel, q_rows), out_shape=jax.ShapeDtyp...  59.1 us
    unnamed x1, local copies, waits for them, and re-layouts  1.67 us

profile of v3, /device:TPU:96, one launch (start us, length us, event | category | flops | bytes accessed | tf_op | source)
XLA Modules:
  0.0 60.8 jit_solution(7447527981774443558)
XLA Ops:
  0.0 59.1 %residual_kernel.1 = f32[2,2,128,128]{3,2,1,0:T(8,128)} custom-call(s32[2,64]{1,0:T(2,128)} %owned.1, s32[2,2,4]{2,1,0:T(2,128)} %plist.1, bf16[744,2944]{1,0:T(8,128)(2,1)} %bitcast.1, bf16[2944,2048]{1,0:T(8,128)(2,1)} %coef.1, bf16[2,2,4,128,128]{4,3,2,1,0:T(8,128)(2,1)} %amp.1), custom_call_target="tpu_custom_call" | custom-call | tf_op jit(solution)/shard_map/residual_kernel/pallas_call | solution.py:407
  59.1 1.7 %copy.7 = f32[2,2,128,128]{3,2,1,0:T(8,128)} copy(f32[2,2,128,128]{3,2,1,0:T(8,128)} %residual_kernel.1) | data formatting | bytes 524288

commit v4 on v3

--- a/solution.py
+++ b/solution.py
@@ -25,6 +25,7 @@
 NSRC = 8
 CB = 256
 QR = T // 4
+Y_FIRST = (False, False, False, False)
 
 
 def dev(x, y, z, c):
@@ -40,7 +41,7 @@
 def kernel(
     q_rows,
     owned, plist, integ, coef, amp, out,
-    lhs, cbuf, acc, ynat, send, recv, rr, offs, offbuf, amp5, ampbuf, res, rsgot, ysend, ygot, fsend,
+    lhs, cbuf, acc, ynat, send, recv, rr, offs, offbuf, amp5, ampbuf, res, rsgot, ysend, ygot4, ysend4, ygot, fsend,
     lsem, csem, gsend, grecv, f1send, f1recv, f2send, f2recv, rssend, rsrecv, yssend, ysrecv,
     fssend, fsrecv, locsem,
 ):
@@ -139,9 +140,13 @@
         near_offs = pltpu.make_async_copy(offs.at[b], offbuf.at[me8], f1recv.at[1, me8])
         return (far_offs, near_offs, is_self), (far, near, is_self)
 
-    def f2_copy(g, d, yy, where):
-        part = ampbuf.at[pl.ds(4 * g, 4), :, quarter_of(yy)]
-        return remote(part, part, f2send.at[g, d - 1], f2recv.at[g, d - 1], where)
+    def f2_copy(g, kind, receive=False):
+        way = 1 - 2 * (kind % 2)
+        back = (kind // 2 + (1 if receive else 0)) * way
+        slots = pl.ds(4 * g, 4) if kind < 2 else pl.ds(4 * g + 2 * (kind - 2), 2)
+        part = ampbuf.at[slots, :, quarter_of((y + 4 - back) % 4)]
+        where = here if receive else dev(x, (y + 4 + way) % 4, z, c)
+        return remote(part, part, f2send.at[g, kind], f2recv.at[g, kind], where)
 
     def f2_start(g):
         for k in (2 * g, 2 * g + 1):
@@ -152,12 +157,18 @@
                 amp.at[0, :, :, quarter], ampbuf.at[pl.ds(2 * k, 2), :, quarter],
                 f1send.at[0, 0, 0], f1recv.at[0, k], here,
             ).wait_recv()
-        for d in range(1, 4):
-            f2_copy(g, d, y, dev(x, (y + d) % 4, z, c)).start()
+        for kind in range(2):
+            f2_copy(g, kind).start()
+
+    def f2_forward(g):
+        for kind in range(2):
+            f2_copy(g, kind, receive=True).wait_recv()
+        for kind in range(2, 4):
+            f2_copy(g, kind).start()
 
     def f2_wait(g):
-        for d in range(1, 4):
-            f2_copy(g, d, (y + 4 - d) % 4, here).wait_recv()
+        for kind in range(2, 4):
+            f2_copy(g, kind, receive=True).wait_recv()
 
     def by_offset(g):
         for e in range(4):
@@ -165,11 +176,11 @@
             for m in range(NOFF):
                 total = None
                 for k in range(4):
-                    row = offbuf[k8, pl.ds(r + k, 1)]
+                    row = jnp.broadcast_to(offbuf[k8, pl.ds(r + k, 1)], (16, T))
                     hit = jnp.where(row == float(m), 1.0, 0.0).astype(BF16)
-                    term = jnp.broadcast_to(hit, (T, T)) * ampbuf[4 * g + e, k]
+                    term = hit[None] * ampbuf[4 * g + e, k].reshape(T // 16, 16, T)
                     total = term if total is None else total + term
-                amp5[4 * g + e, pl.ds(m * T, T)] = total
+                amp5[4 * g + e, pl.ds(m * T, T)] = total.reshape(T, T)
 
     def half(h, n):
         rows_h = CHUNKS[h]
@@ -292,24 +303,38 @@
                 low, weights, preferred_element_type=F32
             )
 
-    def rs_copy(g, d):
+    def first_copy(g, d):
+        if Y_FIRST[g]:
+            src = res.at[pl.ds(4 * g, 4), quarter_of((y + d) % 4)]
+            return remote(
+                src, ygot4.at[g, d - 1], rssend.at[g, d - 1], rsrecv.at[g, d - 1],
+                dev(x, (y + d) % 4, z, c),
+            )
         return remote(
             res.at[4 * g + (o + d) % 4], rsgot.at[g, d - 1], rssend.at[g, d - 1], rsrecv.at[g, d - 1],
             dev((x + d * c) % 4, y, (z + d * (1 - c)) % 4, c),
         )
 
-    def y_copy(g, d):
+    def second_copy(g, d):
+        if Y_FIRST[g]:
+            return remote(
+                ysend4.at[g, (o + d) % 4], ygot.at[g, d - 1], yssend.at[g, d - 1],
+                ysrecv.at[g, d - 1], dev((x + d * c) % 4, y, (z + d * (1 - c)) % 4, c),
+            )
         return remote(
             ysend.at[g, quarter_of((y + d) % 4)], ygot.at[g, d - 1], yssend.at[g, d - 1],
             ysrecv.at[g, d - 1], dev(x, (y + d) % 4, z, c),
         )
 
-    def y_start(g):
-        for d in range(1, 4):
-            rs_copy(g, d).wait_recv()
-        ysend[g] = (res[4 * g + o] + rsgot[g, 0]) + (rsgot[g, 1] + rsgot[g, 2])
-        for d in range(1, 4):
-            y_copy(g, d).start()
+    def second_start(g):
+        for d in range(1, 4):
+            first_copy(g, d).wait_recv()
+        if Y_FIRST[g]:
+            ysend4[g] = (res[pl.ds(4 * g, 4), quarter] + ygot4[g, 0]) + (ygot4[g, 1] + ygot4[g, 2])
+        else:
+            ysend[g] = (res[4 * g + o] + rsgot[g, 0]) + (rsgot[g, 1] + rsgot[g, 2])
+        for d in range(1, 4):
+            second_copy(g, d).start()
 
     def final_copies(g, d):
         dst = out.at[c, o % 2, quarter]
@@ -321,8 +346,9 @@
 
     def final_start(g):
         for d in range(1, 4):
-            y_copy(g, d).wait_recv()
-        fsend[g] = (ysend[g, quarter] + ygot[g, 0]) + (ygot[g, 1] + ygot[g, 2])
+            second_copy(g, d).wait_recv()
+        mine = ysend4[g, o] if Y_FIRST[g] else ysend[g, quarter]
+        fsend[g] = (mine + ygot[g, 0]) + (ygot[g, 1] + ygot[g, 2])
         for d in range(4):
             start_either(final_copies(g, d))
 
@@ -353,22 +379,28 @@
     reorder(1)
     gather_start(1)
     lhs_copy(2).wait()
-    lax.fori_loop(0, nblk, block(2), 0)
+    lax.fori_loop(0, nblk // 2, block(2), 0)
+    f2_forward(0)
+    lax.fori_loop(nblk // 2, nblk, block(2), 0)
     reorder(2)
     gather_start(2)
-    for h in range(NCH - 1):
-        gather_wait(h, 0)
-    pairs(0, START[-1], 0, BLK // 2)
+    f2_forward(1)
+    gather_wait(0, 0)
+    pairs(0, START[1], 0, BLK // 2)
+    f2_forward(2)
+    f2_forward(3)
+    gather_wait(1, 0)
+    pairs(START[1], START[2], 0, BLK // 2)
     for g in range(4):
+        gather_wait(2, g)
+        pairs(START[2], ROWS, 2 * g, 2 * g + 2)
         f2_wait(g)
         by_offset(g)
-        gather_wait(NCH - 1, g)
-        pairs(START[-1], ROWS, 2 * g, 2 * g + 2)
         contract(g)
         for d in range(1, 4):
-            rs_copy(g, d).start()
+            first_copy(g, d).start()
     for g in range(4):
-        y_start(g)
+        second_start(g)
     for g in range(4):
         final_start(g)
 
@@ -389,10 +421,11 @@
             for copy in gather_copies(h, g)[0]:
                 copy.wait_send()
     for g in range(4):
-        for d in range(1, 4):
-            f2_copy(g, d, y, here).wait_send()
-            rs_copy(g, d).wait_send()
-            y_copy(g, d).wait_send()
+        for kind in range(4):
+            f2_copy(g, kind).wait_send()
+        for d in range(1, 4):
+            first_copy(g, d).wait_send()
+            second_copy(g, d).wait_send()
         for d in range(4):
             finish_send(final_copies(g, d))
 
@@ -407,7 +440,7 @@
     return pl.pallas_call(
         functools.partial(kernel, q_rows),
         out_shape=jax.ShapeDtypeStruct((NB, 2, T, T), F32),
-        in_specs=[smem, smem, hbm, hbm, vmem],
+        in_specs=[smem, smem, hbm, hbm, hbm],
         out_specs=vmem,
         scratch_shapes=[
             pltpu.VMEM((ROWS * NOCC, ao), BF16),
@@ -424,6 +457,8 @@
             pltpu.VMEM((BLK, T, T), F32),
             pltpu.VMEM((4, 3, T, T), F32),
             pltpu.VMEM((4, T, T), F32),
+            pltpu.VMEM((4, 3, 4, QR, T), F32),
+            pltpu.VMEM((4, 4, QR, T), F32),
             pltpu.VMEM((4, 3, QR, T), F32),
             pltpu.VMEM((4, QR, T), F32),
             dma((NCH,)),
@@ -432,8 +467,8 @@
             dma((NCH + 3, NSRC)),
             dma((2, NB, 4)),
             dma((2, NSRC)),
-            dma((4, 3)),
-            dma((4, 3)),
+            dma((4, 4)),
+            dma((4, 4)),
             dma((4, 3)),
             dma((4, 3)),
             dma((4, 3)),

time: 61.1 us -> 59.3 us (0.971)
  Pallas kernels: 59.1 us -> 57.5 us
    pallas_call x1, Pallas kernels: 59.1 us -> 57.5 us  [per_device(): pl.pallas_call(functools.partial(kernel, q_rows), out_shape=jax.ShapeDtyp...]
where the time goes in v4:
time: 59.3 us; the launch traced here: 59.2 us
  Pallas kernels  57.5 us (97%)
  local copies, waits for them, and re-layouts  1.67 us (3%)
    pallas_call x1, Pallas kernels, per_device(): pl.pallas_call(functools.partial(kernel, q_rows), out_shape=jax.ShapeDtyp...  57.5 us
    unnamed x1, local copies, waits for them, and re-layouts  1.67 us

profile of v4, /device:TPU:96, one launch (start us, length us, event | category | flops | bytes accessed | tf_op | source)
XLA Modules:
  0.0 59.2 jit_solution(538390857333628167)
XLA Ops:
  0.0 57.5 %residual_kernel.1 = f32[2,2,128,128]{3,2,1,0:T(8,128)} custom-call(s32[2,64]{1,0:T(2,128)} %owned.1, s32[2,2,4]{2,1,0:T(2,128)} %plist.1, bf16[744,2944]{1,0:T(8,128)(2,1)} %bitcast.1, bf16[2944,2048]{1,0:T(8,128)(2,1)} %coef.1, bf16[2,2,4,128,128]{4,3,2,1,0:T(8,128)(2,1)} %amp.1), custom_call_target="tpu_custom_call" | custom-call | tf_op jit(solution)/shard_map/residual_kernel/pallas_call | solution.py:440
  57.5 1.7 %copy.7 = f32[2,2,128,128]{3,2,1,0:T(8,128)} copy(f32[2,2,128,128]{3,2,1,0:T(8,128)} %residual_kernel.1) | data formatting | bytes 524288

commit v5 on v4

--- a/solution.py
+++ b/solution.py
@@ -25,7 +25,6 @@
 NSRC = 8
 CB = 256
 QR = T // 4
-Y_FIRST = (False, False, False, False)
 
 
 def dev(x, y, z, c):
@@ -41,7 +40,7 @@
 def kernel(
     q_rows,
     owned, plist, integ, coef, amp, out,
-    lhs, cbuf, acc, ynat, send, recv, rr, offs, offbuf, amp5, ampbuf, res, rsgot, ysend, ygot4, ysend4, ygot, fsend,
+    lhs, cbuf, acc, ynat, send, recv, rr, offs, offbuf, amp5, ampbuf, res, rsgot, ysend, ygot, fsend,
     lsem, csem, gsend, grecv, f1send, f1recv, f2send, f2recv, rssend, rsrecv, yssend, ysrecv,
     fssend, fsrecv, locsem,
 ):
@@ -304,23 +303,12 @@
             )
 
     def first_copy(g, d):
-        if Y_FIRST[g]:
-            src = res.at[pl.ds(4 * g, 4), quarter_of((y + d) % 4)]
-            return remote(
-                src, ygot4.at[g, d - 1], rssend.at[g, d - 1], rsrecv.at[g, d - 1],
-                dev(x, (y + d) % 4, z, c),
-            )
         return remote(
             res.at[4 * g + (o + d) % 4], rsgot.at[g, d - 1], rssend.at[g, d - 1], rsrecv.at[g, d - 1],
             dev((x + d * c) % 4, y, (z + d * (1 - c)) % 4, c),
         )
 
     def second_copy(g, d):
-        if Y_FIRST[g]:
-            return remote(
-                ysend4.at[g, (o + d) % 4], ygot.at[g, d - 1], yssend.at[g, d - 1],
-                ysrecv.at[g, d - 1], dev((x + d * c) % 4, y, (z + d * (1 - c)) % 4, c),
-            )
         return remote(
             ysend.at[g, quarter_of((y + d) % 4)], ygot.at[g, d - 1], yssend.at[g, d - 1],
             ysrecv.at[g, d - 1], dev(x, (y + d) % 4, z, c),
@@ -329,10 +317,7 @@
     def second_start(g):
         for d in range(1, 4):
             first_copy(g, d).wait_recv()
-        if Y_FIRST[g]:
-            ysend4[g] = (res[pl.ds(4 * g, 4), quarter] + ygot4[g, 0]) + (ygot4[g, 1] + ygot4[g, 2])
-        else:
-            ysend[g] = (res[4 * g + o] + rsgot[g, 0]) + (rsgot[g, 1] + rsgot[g, 2])
+        ysend[g] = (res[4 * g + o] + rsgot[g, 0]) + (rsgot[g, 1] + rsgot[g, 2])
         for d in range(1, 4):
             second_copy(g, d).start()
 
@@ -347,8 +332,7 @@
     def final_start(g):
         for d in range(1, 4):
             second_copy(g, d).wait_recv()
-        mine = ysend4[g, o] if Y_FIRST[g] else ysend[g, quarter]
-        fsend[g] = (mine + ygot[g, 0]) + (ygot[g, 1] + ygot[g, 2])
+        fsend[g] = (ysend[g, quarter] + ygot[g, 0]) + (ygot[g, 1] + ygot[g, 2])
         for d in range(4):
             start_either(final_copies(g, d))
 
@@ -392,10 +376,10 @@
     gather_wait(1, 0)
     pairs(START[1], START[2], 0, BLK // 2)
     for g in range(4):
+        f2_wait(g)
+        by_offset(g)
         gather_wait(2, g)
         pairs(START[2], ROWS, 2 * g, 2 * g + 2)
-        f2_wait(g)
-        by_offset(g)
         contract(g)
         for d in range(1, 4):
             first_copy(g, d).start()
@@ -457,8 +441,6 @@
             pltpu.VMEM((BLK, T, T), F32),
             pltpu.VMEM((4, 3, T, T), F32),
             pltpu.VMEM((4, T, T), F32),
-            pltpu.VMEM((4, 3, 4, QR, T), F32),
-            pltpu.VMEM((4, 4, QR, T), F32),
             pltpu.VMEM((4, 3, QR, T), F32),
             pltpu.VMEM((4, QR, T), F32),
             dma((NCH,)),

time: 59.3 us -> 59.1 us (level)
  no operation moved by 1% of the time
where the time goes in v5:
time: 59.1 us; the launch traced here: 58.9 us
  Pallas kernels  57.2 us (97%)
  local copies, waits for them, and re-layouts  1.67 us (3%)
    pallas_call x1, Pallas kernels, per_device(): pl.pallas_call(functools.partial(kernel, q_rows), out_shape=jax.ShapeDtyp...  57.2 us
    unnamed x1, local copies, waits for them, and re-layouts  1.67 us

profile of v5, /device:TPU:96, one launch (start us, length us, event | category | flops | bytes accessed | tf_op | source)
XLA Modules:
  0.0 58.9 jit_solution(8074477696922264255)
XLA Ops:
  0.0 57.2 %residual_kernel.1 = f32[2,2,128,128]{3,2,1,0:T(8,128)} custom-call(s32[2,64]{1,0:T(2,128)} %owned.1, s32[2,2,4]{2,1,0:T(2,128)} %plist.1, bf16[744,2944]{1,0:T(8,128)(2,1)} %bitcast.1, bf16[2944,2048]{1,0:T(8,128)(2,1)} %coef.1, bf16[2,2,4,128,128]{4,3,2,1,0:T(8,128)(2,1)} %amp.1), custom_call_target="tpu_custom_call" | custom-call | tf_op jit(solution)/shard_map/residual_kernel/pallas_call | solution.py:424
  57.2 1.7 %copy.7 = f32[2,2,128,128]{3,2,1,0:T(8,128)} copy(f32[2,2,128,128]{3,2,1,0:T(8,128)} %residual_kernel.1) | data formatting | bytes 524288

commit v6 on v5

--- a/solution.py
+++ b/solution.py
@@ -429,7 +429,7 @@
         scratch_shapes=[
             pltpu.VMEM((ROWS * NOCC, ao), BF16),
             pltpu.VMEM((nv // CB, ao, CB), BF16),
-            pltpu.VMEM((CB // T, max(CHUNKS) * NOCC, T), F32),
+            pltpu.VMEM((CB // T, (max(CHUNKS) + 1) * NOCC, T), F32),
             pltpu.VMEM((NB, NT, max(CHUNKS), T), BF16),
             pltpu.VMEM((NB, NT + 4, ROWS, T), BF16),
             pltpu.VMEM((WIN, NSRC * ROWS, T), BF16),

time: 59.1 us -> 59.1 us (level)
  no operation moved by 1% of the time
where the time goes in v6:
time: 59.1 us; the launch traced here: 58.9 us
  Pallas kernels  57.2 us (97%)
  local copies, waits for them, and re-layouts  1.67 us (3%)
    pallas_call x1, Pallas kernels, per_device(): pl.pallas_call(functools.partial(kernel, q_rows), out_shape=jax.ShapeDtyp...  57.2 us
    unnamed x1, local copies, waits for them, and re-layouts  1.67 us

profile of v6, /device:TPU:96, one launch (start us, length us, event | category | flops | bytes accessed | tf_op | source)
XLA Modules:
  0.0 58.9 jit_solution(9391417157040163409)
XLA Ops:
  0.0 57.2 %residual_kernel.1 = f32[2,2,128,128]{3,2,1,0:T(8,128)} custom-call(s32[2,64]{1,0:T(2,128)} %owned.1, s32[2,2,4]{2,1,0:T(2,128)} %plist.1, bf16[744,2944]{1,0:T(8,128)(2,1)} %bitcast.1, bf16[2944,2048]{1,0:T(8,128)(2,1)} %coef.1, bf16[2,2,4,128,128]{4,3,2,1,0:T(8,128)(2,1)} %amp.1), custom_call_target="tpu_custom_call" | custom-call | tf_op jit(solution)/shard_map/residual_kernel/pallas_call | solution.py:424
  57.2 1.7 %copy.7 = f32[2,2,128,128]{3,2,1,0:T(8,128)} copy(f32[2,2,128,128]{3,2,1,0:T(8,128)} %residual_kernel.1) | data formatting | bytes 524288

commit v7 on v6

--- a/solution.py
+++ b/solution.py
@@ -346,13 +346,12 @@
         return one
 
     lhs_copy(0).wait()
-    lax.fori_loop(0, 1, block(0), 0)
     pl.semaphore_wait(bar, 22)
     for d in range(4):
         for b in range(NB):
             for one in f1_copies(b, d):
                 start_either(one)
-    lax.fori_loop(1, nblk, block(0), 0)
+    lax.fori_loop(0, nblk, block(0), 0)
     reorder(0)
     gather_start(0)
     lhs_copy(1).wait()

time: 59.1 us -> 58.9 us (level)
  no operation moved by 1% of the time
where the time goes in v7:
time: 58.9 us; the launch traced here: 58.8 us
  Pallas kernels  57.1 us (97%)
  local copies, waits for them, and re-layouts  1.67 us (3%)
    pallas_call x1, Pallas kernels, per_device(): pl.pallas_call(functools.partial(kernel, q_rows), out_shape=jax.ShapeDtyp...  57.1 us
    unnamed x1, local copies, waits for them, and re-layouts  1.67 us

profile of v7, /device:TPU:96, one launch (start us, length us, event | category | flops | bytes accessed | tf_op | source)
XLA Modules:
  0.0 58.8 jit_solution(9638225070072995770)
XLA Ops:
  0.0 57.1 %residual_kernel.1 = f32[2,2,128,128]{3,2,1,0:T(8,128)} custom-call(s32[2,64]{1,0:T(2,128)} %owned.1, s32[2,2,4]{2,1,0:T(2,128)} %plist.1, bf16[744,2944]{1,0:T(8,128)(2,1)} %bitcast.1, bf16[2944,2048]{1,0:T(8,128)(2,1)} %coef.1, bf16[2,2,4,128,128]{4,3,2,1,0:T(8,128)(2,1)} %amp.1), custom_call_target="tpu_custom_call" | custom-call | tf_op jit(solution)/shard_map/residual_kernel/pallas_call | solution.py:423
  57.1 1.7 %copy.7 = f32[2,2,128,128]{3,2,1,0:T(8,128)} copy(f32[2,2,128,128]{3,2,1,0:T(8,128)} %residual_kernel.1) | data formatting | bytes 524288
